TPU v7x, 32 devices: a whole 2x2x4 slice. The times are simulated.
32 devices in a mesh: energy: 8 (over y, x, core), cuts: 4 (over z).
Axes of the slice: x: 2, y: 2, z: 4, core: 2. Of those that a mesh axis runs over, the one named last changes fastest.
Arguments:
- green_diag: bfloat16 [4, 32, 2, 256, 256], P('cuts', 'energy'), may hold values from -0.375 to 0.375
- green_upper: bfloat16 [4, 32, 2, 256, 256], P('cuts', 'energy'), may hold values from -0.375 to 0.375
- sigma_lesser: bfloat16 [4, 32, 2, 256, 256], P('cuts', 'energy'), may hold values from -6 to 6
- screening: bfloat16 [4, 32, 2, 256, 256], P('cuts', 'energy'), may hold values from -0.375 to 0.375
Outputs:
- polar_screened: bfloat16 [4, 32, 2, 256, 256], P('cuts', 'energy')
All inputs are finite; a program needn't handle non-finite values.
Results may differ from a plain program's by a relative error of at most 0.013.
Values may be sent and summed in bfloat16 or wider, within the bound.
A program may use at most 64 MiB of HBM per device.

v0:
```python
import math

import jax
import jax.numpy as jnp
from jax import lax
from jax.sharding import PartitionSpec as P


def shifted(value, axis, steps):
    count = lax.axis_size(axis)
    leading, last = (max(0, -steps), min(count, count - steps))
    return lax.ppermute(value, axis, [(source, source + steps) for source in range(leading, last)])


def times_block(left, right):
    real = jnp.einsum(
        "eij,ejk->eik", left[:, 0], right[:, 0], preferred_element_type=jnp.float32
    ) - jnp.einsum("eij,ejk->eik", left[:, 1], right[:, 1], preferred_element_type=jnp.float32)
    imag = jnp.einsum(
        "eij,ejk->eik", left[:, 0], right[:, 1], preferred_element_type=jnp.float32
    ) + jnp.einsum("eij,ejk->eik", left[:, 1], right[:, 0], preferred_element_type=jnp.float32)
    return jnp.stack([real, imag], axis=1)


def times_adjoint(left, right):
    real = jnp.einsum(
        "eij,ekj->eik", left[:, 0], right[:, 0], preferred_element_type=jnp.float32
    ) + jnp.einsum("eij,ekj->eik", left[:, 1], right[:, 1], preferred_element_type=jnp.float32)
    imag = jnp.einsum(
        "eij,ekj->eik", left[:, 1], right[:, 0], preferred_element_type=jnp.float32
    ) - jnp.einsum("eij,ekj->eik", left[:, 0], right[:, 1], preferred_element_type=jnp.float32)
    return jnp.stack([real, imag], axis=1)


def angle_table(rows_count, cols_count, period):
    row_index = lax.broadcasted_iota(jnp.int32, (rows_count, cols_count), 0)
    col_index = lax.broadcasted_iota(jnp.int32, (rows_count, cols_count), 1)
    phase = (row_index * col_index % period).astype(jnp.float32)
    return phase * (2.0 * math.pi / period)


def split_table_dot(table, data):
    upper = table.astype(jnp.bfloat16)
    lower = (table - upper.astype(jnp.float32)).astype(jnp.bfloat16)
    return jnp.dot(upper, data, preferred_element_type=jnp.float32) + jnp.dot(
        lower, data, preferred_element_type=jnp.float32
    )


def correlate(spread):
    energies = spread.shape[0]
    period = 2 * energies
    forward = angle_table(period, energies, period)
    inverse = angle_table(energies, period, period)
    cos_inv = jnp.cos(inverse)
    sin_inv = jnp.sin(inverse)
    high = lax.Precision.HIGHEST
    real_part = spread[:, 0].reshape(energies, -1)
    imag_part = spread[:, 1].reshape(energies, -1)
    width = real_part.shape[1]
    joined = jnp.concatenate([real_part, imag_part], axis=1)
    cos_both = split_table_dot(jnp.cos(forward), joined)
    sin_both = split_table_dot(jnp.sin(forward), joined)
    spec_real = cos_both[:, :width] + sin_both[:, width:]
    spec_imag = cos_both[:, width:] - sin_both[:, :width]
    power = spec_real * spec_real + spec_imag * spec_imag
    lag_real = jnp.dot(cos_inv, power, precision=high) / period
    lag_imag = jnp.dot(sin_inv, power, precision=high) / period
    polar = jnp.stack([lag_real, lag_imag], axis=1) / energies
    return polar.reshape(spread.shape).astype(jnp.bfloat16)


def shards(green_diag, green_upper, sigma_lesser, screening):
    sigma_next = shifted(sigma_lesser, "cuts", -1)
    own_term = times_block(green_diag[0], sigma_lesser[0]).astype(jnp.bfloat16)
    pair_term = times_block(green_upper[0], sigma_next[0]).astype(jnp.bfloat16)
    lesser = (
        times_adjoint(own_term, green_diag[0]) + times_adjoint(pair_term, green_upper[0])
    ).astype(jnp.bfloat16)
    entries = lax.all_to_all(lesser, "energy", split_axis=2, concat_axis=0, tiled=True)
    polar_rows = correlate(entries)
    back_field = lax.all_to_all(polar_rows, "energy", split_axis=0, concat_axis=2, tiled=True)
    screened_left = times_block(screening[0], back_field).astype(jnp.bfloat16)
    result_field = times_adjoint(screened_left, screening[0]).astype(jnp.bfloat16)
    return result_field[None]


def solution(mesh):
    in_specs = (
        P("cuts", "energy", None, None, None),
        P("cuts", "energy", None, None, None),
        P("cuts", "energy", None, None, None),
        P("cuts", "energy", None, None, None),
    )
    out_specs = P("cuts", "energy", None, None, None)
    return jax.shard_map(shards, mesh=mesh, in_specs=in_specs, out_specs=out_specs, check_vma=False)
```

profile of v0, /device:TPU:0, one launch (start us, length us, event | category | flops | bytes accessed | tf_op | source)
XLA Modules:
  0.0 84.3 jit_solution(1953093069969859186)
XLA Ops:
  0.0 1.4 %copy.97 = bf16[1,4,2,256,256]{4,3,1,2,0:T(8,128)(2,1)S(1)} copy(bf16[1,4,2,256,256]{4,3,2,1,0:T(8,128)(2,1)} %param.6) | data formatting | bytes 2097152 | tf_op args[2]
  1.4 1.3 %collective-permute-start = (bf16[1,4,2,256,256]{4,3,1,2,0:T(8,128)(2,1)S(1)}, bf16[1,4,2,256,256]{4,3,1,2,0:T(8,128)(2,1)S(1)}, u32[]{:S(2)}, u32[]{:S(2)}) collective-permute-start(bf16[1,4,2,256,256]{4,3,1,2,0:T(8,128)(2,1)S(1)} %copy.97), channel_id=1, source_target_pairs={{1,0},{2,1},{3,2},{5,4},{6,5},{7,6},{9,8},{10,9},{11,10},{13,12},{... | collective-permute-start | bytes 3145736 | tf_op jit(solution)/shard_map/ppermute | solution.py:12
  4.0 0.6 copy-done.1
  6.0 23.5 %collective-permute-done = bf16[1,4,2,256,256]{4,3,1,2,0:T(8,128)(2,1)S(1)} collective-permute-done((bf16[1,4,2,256,256]{4,3,1,2,0:T(8,128)(2,1)S(1)}, bf16[1,4,2,256,256]{4,3,1,2,0:T(8,128)(2,1)S(1)}, u32[]{:S(2)}, u32[]{:S(2)}) %collective-permute-start) | collective-permute-done | bytes 1048608 | tf_op jit(solution)/shard_map/ppermute | solution.py:12
  32.1 0.4 fusion.3
  32.5 0.8 copy.65
  33.3 19.0 %all_to_all.36 = bf16[4,2,256,256]{3,0,1,2:T(4,128)(2,1)S(1)} all-to-all(bf16[4,2,256,256]{3,0,1,2:T(4,128)(2,1)S(1)} %copy.65), channel_id=1, replica_groups=mesh['energy'=8,'cuts'=4] {'energy'}, dimensions={2} | all-to-all | bytes 2097152 | tf_op jit(solution)/shard_map/all_to_all | solution.py:80
  53.4 0.8 fusion.51
  54.2 0.8 fusion.48
  55.0 0.8 convolution_add_fusion.1
  55.9 0.8 convolution_add_fusion
  56.7 0.4 fusion.1
  57.1 1.2 %convolution_multiply_fusion.1 = f32[32,8192]{1,0:T(8,128)S(1)} fusion(f32[64,8192]{1,0:T(8,128)S(1)} %fusion.1), kind=kOutput, calls=%fused_computation.3 | convolution fusion | flops 201617408 | bytes 3145728 | tf_op jit(solution)/shard_map/dot_general | solution.py:67
  58.3 1.2 %convolution_multiply_fusion = f32[32,8192]{1,0:T(8,128)S(1)} fusion(f32[64,8192]{1,0:T(8,128)S(1)} %fusion.1), kind=kOutput, calls=%fused_computation.2 | convolution fusion | flops 201617408 | bytes 3145728 | tf_op jit(solution)/shard_map/dot_general | solution.py:68
  60.1 1.3 %fusion.4 = bf16[32,2,32,256]{3,2,1,0:T(8,128)(2,1)} fusion(f32[32,1,32,256]{3,2,1,0:T(8,128)S(1)} %bitcast.167, f32[32,1,32,256]{3,2,1,0:T(8,128)S(1)} %bitcast.165), kind=kLoop, calls=%fused_computation.12 | loop fusion | flops 1572864 | bytes 3145728 | tf_op jit(solution)/shard_map/convert_element_type | solution.py:70
  61.4 3.6 %all-to-all-start.1 = ((bf16[32,2,32,256]{3,2,1,0:T(8,128)(2,1)}), bf16[32,2,32,256]{3,2,1,0:T(8,128)(2,1)S(1)}, u32[]{:S(2)}, u32[]{:S(2)}) async-start(bf16[32,2,32,256]{3,2,1,0:T(8,128)(2,1)} %fusion.4), calls=%async_computation.1 | async-start | bytes 2097152 | tf_op jit(solution)/shard_map/all_to_all | solution.py:82
  65.1 15.2 %all-to-all-done.1 = bf16[32,2,32,256]{3,2,1,0:T(8,128)(2,1)S(1)} async-done(((bf16[32,2,32,256]{3,2,1,0:T(8,128)(2,1)}), bf16[32,2,32,256]{3,2,1,0:T(8,128)(2,1)S(1)}, u32[]{:S(2)}, u32[]{:S(2)}) %all-to-all-start.1) | async-done | bytes 1048608 | tf_op jit(solution)/shard_map/all_to_all | solution.py:82
  80.7 0.3 fusion.24
  81.1 0.3 fusion.13
  81.8 0.3 fusion.14
  82.1 0.3 fusion.29
  82.5 0.4 fusion.18
  82.8 0.3 fusion.17
  83.3 1.0 %copy.78 = bf16[1,4,2,256,256]{4,3,2,1,0:T(8,128)(2,1)} copy(bf16[1,4,2,256,256]{4,3,1,2,0:T(8,128)(2,1)S(1)} %pad_maximum_fusion) | data formatting | bytes 2097152 | tf_op jit(solution)/shard_map/stack | solution.py:32
  (37 shorter events, 7.8 us)
Async XLA Ops:
  0.0 2.7 %copy-start = (bf16[1,4,2,256,256]{4,3,2,1,0:T(8,128)(2,1)S(1)}, bf16[1,4,2,256,256]{4,3,2,1,0:T(8,128)(2,1)}, u32[]{:S(2)}) copy-start(bf16[1,4,2,256,256]{4,3,2,1,0:T(8,128)(2,1)} %param.4) | copy-start | bytes 3145732
  1.4 28.1 %collective-permute-start = (bf16[1,4,2,256,256]{4,3,1,2,0:T(8,128)(2,1)S(1)}, bf16[1,4,2,256,256]{4,3,1,2,0:T(8,128)(2,1)S(1)}, u32[]{:S(2)}, u32[]{:S(2)}) collective-permute-start(bf16[1,4,2,256,256]{4,3,1,2,0:T(8,128)(2,1)S(1)} %copy.97), channel_id=1, source_target_pairs={{1,0},{2,1},{3,2},{5,4},{6,5},{7,6},{9,8},{10,9},{11,10},{13,12},{... | collective-permute-start | bytes 3145736 | tf_op jit(solution)/shard_map/ppermute | solution.py:12
  3.4 1.2 %copy-start.1 = (bf16[1,4,2,256,256]{4,3,2,1,0:T(8,128)(2,1)S(1)}, bf16[1,4,2,256,256]{4,3,2,1,0:T(8,128)(2,1)}, u32[]{:S(2)}) copy-start(bf16[1,4,2,256,256]{4,3,2,1,0:T(8,128)(2,1)} %param.5) | copy-start | bytes 3145732
  60.1 4.9 %copy-start.2 = (bf16[1,4,2,256,256]{4,3,2,1,0:T(8,128)(2,1)S(1)}, bf16[1,4,2,256,256]{4,3,2,1,0:T(8,128)(2,1)}, u32[]{:S(2)}) copy-start(bf16[1,4,2,256,256]{4,3,2,1,0:T(8,128)(2,1)} %param.7) | copy-start | bytes 3145732
  61.4 18.9 %all-to-all-start.1 = ((bf16[32,2,32,256]{3,2,1,0:T(8,128)(2,1)}), bf16[32,2,32,256]{3,2,1,0:T(8,128)(2,1)S(1)}, u32[]{:S(2)}, u32[]{:S(2)}) async-start(bf16[32,2,32,256]{3,2,1,0:T(8,128)(2,1)} %fusion.4), calls=%async_computation.1 | async-start | bytes 2097152 | tf_op jit(solution)/shard_map/all_to_all | solution.py:82
where the time goes:
time: 84.6 us; the launch traced here: 84.3 us
  waiting for transfers between devices  38.7 us (46%)
  blocking collectives  19 us (22%)
  matrix products  13.4 us (16%)
  local copies, waits for them, and re-layouts  5.79 us (7%)
  starting transfers between devices  4.85 us (6%)
  other arithmetic  2.23 us (3%)
    ppermute x1, waiting for transfers between devices, shifted(): lax.ppermute(value, axis, [(source, source + steps) for source in range(l...  23.5 us
    all_to_all x1, blocking collectives, shards(): lax.all_to_all(lesser, 'energy', split_axis=2, concat_axis=0, tiled=True)  19 us
    all_to_all x1, waiting for transfers between devices, shards(): lax.all_to_all(polar_rows, 'energy', split_axis=0, concat_axis=2, tiled=T...  15.2 us
    all_to_all x1, starting transfers between devices, shards(): lax.all_to_all(polar_rows, 'energy', split_axis=0, concat_axis=2, tiled=T...  3.56 us
    unnamed x15, local copies, waits for them, and re-layouts  3.45 us
  transfers between devices with their start and end apart: 2, of which 2 were waited for; matrix products, arithmetic and copies ran while one was open for 3% of the time, Pallas kernels for 0%

commit v1 on v0

v1 whole, which is shorter than its diff:
```python
import functools

import jax
import jax.numpy as jnp
import numpy as np
from jax import lax
from jax.experimental import pallas as pl
from jax.experimental.pallas import tpu as pltpu
from jax.sharding import PartitionSpec as P

LANES = 128
MESH = pl.DeviceIdType.MESH
F32 = jnp.float32
BF16 = jnp.bfloat16


def tables(groups, local):
    energies = groups * local
    period = 2 * energies
    order = np.array([s * local + j for j in range(local) for s in range(groups)])
    freq = np.arange(period)
    angle = 2.0 * np.pi * ((freq[:, None] * order[None, :]) % period) / period
    cos, sin = np.cos(angle), np.sin(angle)
    forward = np.zeros((2 * period, energies, 2))
    forward[:period, :, 0], forward[:period, :, 1] = cos, sin
    forward[period:, :, 0], forward[period:, :, 1] = -sin, cos
    forward = forward.reshape(2 * period, 2 * energies).astype(np.float32)
    inverse = np.stack([cos.T, sin.T], axis=1).reshape(2 * energies, period)
    inverse = (inverse / (period * energies)).astype(np.float32)

    def split(table):
        high = table.astype(BF16)
        return high, (table - high.astype(np.float32)).astype(BF16)

    f_high, f_low = split(forward)
    i_high, i_low = split(inverse)
    return (
        np.concatenate([f_high, f_low], axis=1),
        np.concatenate([i_high, i_high, i_low], axis=1),
    )


def dot(left, right):
    return jnp.dot(left, right, preferred_element_type=F32)


def dot_t(left, right):
    return lax.dot_general(left, right, (((1,), (1,)), ((), ())), preferred_element_type=F32)


def times(lr, li, rr, ri):
    return dot(lr, rr) - dot(li, ri), dot(lr, ri) + dot(li, rr)


def times_adjoint(lr, li, rr, ri):
    return dot_t(lr, rr) + dot_t(li, ri), dot_t(li, rr) - dot_t(lr, ri)


def kernel(
    groups, slices, halves,
    gd_hbm, gu_hbm, s_hbm, w_hbm, fwd_ref, inv_ref, out_hbm,
    gd, gu, sig, scr, snext, own, lbuf, entries, xf, pf, pbuf, back, obuf,
    in_sem, z_send, z_recv, a_send, a_recv, b_send, b_recv, o_sem,
):
    me = lax.axis_index("energy")
    cut = lax.axis_index("cuts")
    local, _, size, _ = gd.shape
    rows = size // groups
    part = rows // halves
    count = 2 * groups * local
    slab = 2 * groups * rows

    barrier = pltpu.get_barrier_semaphore()

    def greet(k, carry):
        pl.semaphore_signal(
            barrier, inc=1, device_id={"energy": lax.rem(me + k, groups)}, device_id_type=MESH
        )
        return carry

    @pl.when(cut > 0)
    def _():
        pl.semaphore_signal(barrier, inc=1, device_id={"cuts": cut - 1}, device_id_type=MESH)

    @pl.when(cut < slices - 1)
    def _():
        pl.semaphore_signal(barrier, inc=1, device_id={"cuts": cut + 1}, device_id_type=MESH)

    lax.fori_loop(1, groups, greet, 0)

    loads = [
        pltpu.make_async_copy(source, target, in_sem.at[i])
        for i, (source, target) in enumerate(
            [(gd_hbm, gd), (s_hbm, sig), (gu_hbm, gu), (w_hbm, scr)]
        )
    ]
    loads[0].start()
    loads[1].start()

    edges = jnp.where(cut > 0, 1, 0) + jnp.where(cut < slices - 1, 1, 0)
    pl.semaphore_wait(barrier, groups - 1 + edges)

    def shift(j):
        return pltpu.make_async_remote_copy(
            src_ref=s_hbm.at[j], dst_ref=snext.at[j],
            send_sem=z_send.at[j], recv_sem=z_recv.at[j],
            device_id={"cuts": cut - 1}, device_id_type=MESH,
        )

    @pl.when(cut > 0)
    def _():
        for j in range(local):
            shift(j).start()

    loads[2].start()
    loads[3].start()
    loads[0].wait()
    loads[1].wait()

    def own_step(j, carry):
        tr, ti = times(gd[j, 0], gd[j, 1], sig[j, 0], sig[j, 1])
        lr, li = times_adjoint(tr.astype(BF16), ti.astype(BF16), gd[j, 0], gd[j, 1])
        own[j, 0] = lr
        own[j, 1] = li
        return carry

    lax.fori_loop(0, local, own_step, 0)
    loads[2].wait()
    loads[3].wait()

    def take(j):
        pltpu.make_async_copy(
            entries.at[j, pl.ds(0, groups - 1)], entries.at[j, pl.ds(0, groups - 1)], a_recv.at[j]
        ).wait()
        wide = entries[j].astype(F32).reshape(slab, size)
        for q in range(size // LANES):
            xf[pl.ds(q * count * rows + j * slab, slab), :] = wide[:, q * LANES : (q + 1) * LANES]

    def lesser_step(j, carry):
        @pl.when(cut < slices - 1)
        def _():
            shift(j).wait_recv()
            tr, ti = times(gu[j, 0], gu[j, 1], snext[j, 0], snext[j, 1])
            lr, li = times_adjoint(tr.astype(BF16), ti.astype(BF16), gu[j, 0], gu[j, 1])
            own[j, 0] += lr
            own[j, 1] += li

        for c in range(2):
            value = own[j, c].astype(BF16).reshape(groups, rows, size)
            lbuf[j, :, c] = value
        entries[j, me] = lbuf[j, me]

        def send(k, inner):
            to = lax.rem(me + k, groups)
            pltpu.make_async_remote_copy(
                src_ref=lbuf.at[j, to], dst_ref=entries.at[j, me],
                send_sem=a_send.at[j], recv_sem=a_recv.at[j],
                device_id={"energy": to}, device_id_type=MESH,
            ).start()
            return inner

        lax.fori_loop(1, groups, send, 0)

        @pl.when(j > 0)
        def _():
            take(j - 1)

        return carry

    lax.fori_loop(0, local, lesser_step, 0)
    take(local - 1)

    period = count

    for h in range(halves):

        def correlate(i, carry):
            r = h * part + i
            x = jnp.concatenate(
                [xf[pl.ds(q * count * rows + r, count, stride=rows), :] for q in range(size // LANES)],
                axis=1,
            ).astype(BF16)
            spec = dot(fwd_ref[...], jnp.concatenate([x, x], axis=0))
            re, im = spec[:period], spec[period:]
            power = re * re + im * im
            high = power.astype(BF16)
            low = (power - high.astype(F32)).astype(BF16)
            lag = dot(inv_ref[...], jnp.concatenate([high, low, high], axis=0))
            for q in range(size // LANES):
                pf[pl.ds(q * count * rows + r, count, stride=rows), :] = lag[:, q * LANES : (q + 1) * LANES]
            return carry

        lax.fori_loop(0, part, correlate, 0, unroll=4)

        def ship(j, carry):
            lags = jnp.concatenate(
                [pf[pl.ds(q * count * rows + j * slab, slab), :] for q in range(size // LANES)], axis=1
            )
            lags = lags.reshape(groups, 2, rows, size)[:, :, h * part : (h + 1) * part]
            pbuf[h, j] = lags.astype(BF16)
            back[j, me, h] = pbuf[h, j, me]

            def send(k, inner):
                to = lax.rem(me + k, groups)
                pltpu.make_async_remote_copy(
                    src_ref=pbuf.at[h, j, to], dst_ref=back.at[j, me, h],
                    send_sem=b_send.at[h, j], recv_sem=b_recv.at[h, j],
                    device_id={"energy": to}, device_id_type=MESH,
                ).start()
                return inner

            lax.fori_loop(1, groups, send, 0)
            return carry

        lax.fori_loop(0, local, ship, 0)

    def result_step(j, carry):
        for h in range(halves):
            landed = back.at[j, pl.ds(0, groups - 1), h]
            pltpu.make_async_copy(landed, landed, b_recv.at[h, j]).wait()
        pr = back[j, :, :, 0].reshape(size, size)
        pi = back[j, :, :, 1].reshape(size, size)
        tr, ti = times(scr[j, 0], scr[j, 1], pr, pi)
        lr, li = times_adjoint(tr.astype(BF16), ti.astype(BF16), scr[j, 0], scr[j, 1])
        obuf[j, 0] = lr.astype(BF16)
        obuf[j, 1] = li.astype(BF16)
        pltpu.make_async_copy(obuf.at[j], out_hbm.at[j], o_sem.at[j]).start()
        return carry

    lax.fori_loop(0, local, result_step, 0)

    @pl.when(cut > 0)
    def _():
        for j in range(local):
            shift(j).wait_send()

    for j in range(local):
        sent = lbuf.at[j, pl.ds(0, groups - 1)]
        pltpu.make_async_copy(sent, sent, a_send.at[j]).wait()
        for h in range(halves):
            sent = pbuf.at[h, j, pl.ds(0, groups - 1)]
            pltpu.make_async_copy(sent, sent, b_send.at[h, j]).wait()
        pltpu.make_async_copy(obuf.at[j], out_hbm.at[j], o_sem.at[j]).wait()


def solution(mesh):
    groups, slices = mesh.shape["energy"], mesh.shape["cuts"]

    def shards(green_diag, green_upper, sigma_lesser, screening):
        shape = green_diag.shape[1:]
        local, _, size, _ = shape
        rows = size // groups
        halves = max(1, rows // 16)
        part = rows // halves
        count = 2 * groups * local
        forward, inverse = tables(groups, local)
        block = pltpu.VMEM(shape, BF16)
        dma = pltpu.SemaphoreType.DMA
        anywhere = pl.BlockSpec(memory_space=pl.ANY)
        vmem = pl.BlockSpec(memory_space=pltpu.VMEM)
        result = pl.pallas_call(
            functools.partial(kernel, groups, slices, halves),
            out_shape=jax.ShapeDtypeStruct(shape, BF16),
            in_specs=[anywhere] * 4 + [vmem] * 2,
            out_specs=anywhere,
            scratch_shapes=[
                block, block, block, block, block,
                pltpu.VMEM(shape, F32),
                pltpu.VMEM((local, groups, 2, rows, size), BF16),
                pltpu.VMEM((local, groups, 2, rows, size), BF16),
                pltpu.VMEM((size // LANES * count * rows, LANES), F32),
                pltpu.VMEM((size // LANES * count * rows, LANES), F32),
                pltpu.VMEM((halves, local, groups, 2, part, size), BF16),
                pltpu.VMEM((local, groups, halves, 2, part, size), BF16),
                block,
                dma((4,)),
                dma((local,)), dma((local,)),
                dma((local,)), dma((local,)),
                dma((halves, local)), dma((halves, local)),
                dma((local,)),
            ],
            compiler_params=pltpu.CompilerParams(
                collective_id=0, has_side_effects=True, vmem_limit_bytes=48 * 1024 * 1024
            ),
        )(
            green_diag[0], green_upper[0], sigma_lesser[0], screening[0],
            jnp.asarray(forward), jnp.asarray(inverse),
        )
        return result[None]

    spec = P("cuts", "energy", None, None, None)
    return jax.shard_map(
        shards, mesh=mesh, in_specs=(spec,) * 4, out_specs=spec, check_vma=False
    )
```

time: 84.6 us -> 60.8 us (0.72)
  Pallas kernels: 0 us -> 53 us
  waiting for transfers between devices: 38.7 us -> 0 us
  blocking collectives: 19 us -> 0 us
  matrix products: 13.4 us -> 0 us
  starting transfers between devices: 4.85 us -> 0 us
  other arithmetic: 2.23 us -> 0 us
  local copies, waits for them, and re-layouts: 5.79 us -> 7.38 us
    pallas_call x0 -> x1, Pallas kernels: none -> 53 us  [shards(): pl.pallas_call(functools.partial(kernel, groups, slices, halves), out_sha...]
    ppermute x1 -> x0, waiting for transfers between devices: 23.5 us -> none  [shifted(): lax.ppermute(value, axis, [(source, source + steps) for source in range(l...]
    all_to_all x1 -> x0, blocking collectives: 19 us -> none  [shards(): lax.all_to_all(lesser, 'energy', split_axis=2, concat_axis=0, tiled=True)]
    all_to_all x1 -> x0, waiting for transfers between devices: 15.2 us -> none  [shards(): lax.all_to_all(polar_rows, 'energy', split_axis=0, concat_axis=2, tiled=T...]
    dot_general x30 -> x0, matrix products: 13.4 us -> none  [the longest x2 1.61 us: split_table_dot(): jnp.dot(lower, data, preferred_element_type=jnp.float32)]
    unnamed x15 -> x13, local copies, waits for them, and re-layouts: 3.45 us -> 7.38 us
    all_to_all x1 -> x0, starting transfers between devices: 3.56 us -> none  [shards(): lax.all_to_all(polar_rows, 'energy', split_axis=0, concat_axis=2, tiled=T...]
    convert_element_type x2 -> x0, other arithmetic: 1.72 us -> none  [the longest x1 1.29 us: correlate(): return polar.reshape(spread.shape).astype(jnp.bfloat16)]
  transfers between devices with their start and end apart: 2 -> 0, of which waited for: 2 -> 0; matrix products, arithmetic and copies ran while one was open for 3% -> 0% of each run, Pallas kernels for 0% -> 0%
where the time goes in v1:
time: 60.8 us; the launch traced here: 60.4 us
  Pallas kernels  53 us (87%)
  local copies, waits for them, and re-layouts  7.38 us (12%)
    pallas_call x1, Pallas kernels, shards(): pl.pallas_call(functools.partial(kernel, groups, slices, halves), out_sha...  53 us
    unnamed x13, local copies, waits for them, and re-layouts  7.38 us

profile of v1, /device:TPU:0, one launch (start us, length us, event | category | flops | bytes accessed | tf_op | source)
XLA Modules:
  0.0 60.4 jit_solution(10889607036725910728)
XLA Ops:
  0.0 0.0 copy-start
  0.0 1.2 %copy-done = bf16[1,4,2,256,256]{4,3,2,1,0:T(8,128)(2,1)S(1)} copy-done((bf16[1,4,2,256,256]{4,3,2,1,0:T(8,128)(2,1)S(1)}, bf16[1,4,2,256,256]{4,3,2,1,0:T(8,128)(2,1)}, u32[]{:S(2)}) %copy-start) | copy-done | bytes 1048600
  1.2 0.0 copy-start.1
  1.2 1.2 %copy-done.1 = bf16[1,4,2,256,256]{4,3,2,1,0:T(8,128)(2,1)S(1)} copy-done((bf16[1,4,2,256,256]{4,3,2,1,0:T(8,128)(2,1)S(1)}, bf16[1,4,2,256,256]{4,3,2,1,0:T(8,128)(2,1)}, u32[]{:S(2)}) %copy-start.1) | copy-done | bytes 1048600
  2.5 0.0 copy-start.2
  2.5 1.2 %copy-done.2 = bf16[1,4,2,256,256]{4,3,2,1,0:T(8,128)(2,1)S(1)} copy-done((bf16[1,4,2,256,256]{4,3,2,1,0:T(8,128)(2,1)S(1)}, bf16[1,4,2,256,256]{4,3,2,1,0:T(8,128)(2,1)}, u32[]{:S(2)}) %copy-start.2) | copy-done | bytes 1048600
  3.7 0.0 copy-start.3
  3.7 1.2 %copy-done.3 = bf16[1,4,2,256,256]{4,3,2,1,0:T(8,128)(2,1)S(1)} copy-done((bf16[1,4,2,256,256]{4,3,2,1,0:T(8,128)(2,1)S(1)}, bf16[1,4,2,256,256]{4,3,2,1,0:T(8,128)(2,1)}, u32[]{:S(2)}) %copy-start.3) | copy-done | bytes 1048600
  4.9 0.0 copy-start.4
  4.9 0.8 %copy-done.4 = bf16[64,192]{1,0:T(8,128)(2,1)S(1)} copy-done((bf16[64,192]{1,0:T(8,128)(2,1)S(1)}, bf16[64,192]{1,0:T(8,128)(2,1)}, u32[]{:S(2)}) %copy-start.4) | copy-done | bytes 24600
  5.7 0.0 copy-start.5
  5.7 0.8 %copy-done.5 = bf16[128,128]{1,0:T(8,128)(2,1)S(1)} copy-done((bf16[128,128]{1,0:T(8,128)(2,1)S(1)}, bf16[128,128]{1,0:T(8,128)(2,1)}, u32[]{:S(2)}) %copy-start.5) | copy-done | bytes 32792
  6.4 53.0 %shard_map.64 = bf16[4,2,256,256]{3,2,1,0:T(8,128)(2,1)S(1)} custom-call(bf16[4,2,256,256]{3,2,1,0:T(8,128)(2,1)S(1)} %bitcast.6, bf16[4,2,256,256]{3,2,1,0:T(8,128)(2,1)S(1)} %bitcast.7, bf16[4,2,256,256]{3,2,1,0:T(8,128)(2,1)S(1)} %bitcast.8, bf16[4,2,256,256]{3,2,1,0:T(8,128)(2,1)S(1)} %bitcast.9, bf16[128,128]{1,0:T(8,128)(2,1)S(1)} %copy-done.5, ...), custom_call_target="tpu_custom_call" | custom-call | tf_op jit(solution)/shard_map/pallas_call | solution.py:261
  59.4 1.0 %copy.8 = bf16[1,4,2,256,256]{4,3,2,1,0:T(8,128)(2,1)} copy(bf16[1,4,2,256,256]{4,3,2,1,0:T(8,128)(2,1)S(1)} %bitcast.5) | data formatting | bytes 2097152
Async XLA Ops:
  0.0 1.2 %copy-start = (bf16[1,4,2,256,256]{4,3,2,1,0:T(8,128)(2,1)S(1)}, bf16[1,4,2,256,256]{4,3,2,1,0:T(8,128)(2,1)}, u32[]{:S(2)}) copy-start(bf16[1,4,2,256,256]{4,3,2,1,0:T(8,128)(2,1)} %param.6) | copy-start | bytes 3145732
  1.2 1.2 %copy-start.1 = (bf16[1,4,2,256,256]{4,3,2,1,0:T(8,128)(2,1)S(1)}, bf16[1,4,2,256,256]{4,3,2,1,0:T(8,128)(2,1)}, u32[]{:S(2)}) copy-start(bf16[1,4,2,256,256]{4,3,2,1,0:T(8,128)(2,1)} %param.7) | copy-start | bytes 3145732
  2.5 1.2 %copy-start.2 = (bf16[1,4,2,256,256]{4,3,2,1,0:T(8,128)(2,1)S(1)}, bf16[1,4,2,256,256]{4,3,2,1,0:T(8,128)(2,1)}, u32[]{:S(2)}) copy-start(bf16[1,4,2,256,256]{4,3,2,1,0:T(8,128)(2,1)} %param.8) | copy-start | bytes 3145732
  3.7 1.2 %copy-start.3 = (bf16[1,4,2,256,256]{4,3,2,1,0:T(8,128)(2,1)S(1)}, bf16[1,4,2,256,256]{4,3,2,1,0:T(8,128)(2,1)}, u32[]{:S(2)}) copy-start(bf16[1,4,2,256,256]{4,3,2,1,0:T(8,128)(2,1)} %param.9) | copy-start | bytes 3145732
  4.9 0.8 %copy-start.4 = (bf16[64,192]{1,0:T(8,128)(2,1)S(1)}, bf16[64,192]{1,0:T(8,128)(2,1)}, u32[]{:S(2)}) copy-start(bf16[64,192]{1,0:T(8,128)(2,1)} %constant.5.clone.inv_ref) | copy-start | bytes 73732
  5.7 0.8 %copy-start.5 = (bf16[128,128]{1,0:T(8,128)(2,1)S(1)}, bf16[128,128]{1,0:T(8,128)(2,1)}, u32[]{:S(2)}) copy-start(bf16[128,128]{1,0:T(8,128)(2,1)} %constant.4.clone.fwd_ref) | copy-start | bytes 98308

commit v2 on v1

--- a/solution.py
+++ b/solution.py
@@ -58,8 +58,8 @@
 
 def kernel(
     groups, slices, halves,
-    gd_hbm, gu_hbm, s_hbm, w_hbm, fwd_ref, inv_ref, out_hbm,
-    gd, gu, sig, scr, snext, own, lbuf, entries, xf, pf, pbuf, back, obuf,
+    gd_hbm, gu_hbm, s_hbm, w_hbm, fwd_hbm, inv_hbm, out_hbm,
+    fwd_ref, inv_ref,    gd, gu, sig, scr, snext, own, lbuf, entries, xf, pf, pbuf, back, obuf,
     in_sem, z_send, z_recv, a_send, a_recv, b_send, b_recv, o_sem,
 ):
     me = lax.axis_index("energy")
@@ -91,7 +91,7 @@
     loads = [
         pltpu.make_async_copy(source, target, in_sem.at[i])
         for i, (source, target) in enumerate(
-            [(gd_hbm, gd), (s_hbm, sig), (gu_hbm, gu), (w_hbm, scr)]
+            [(gd_hbm, gd), (s_hbm, sig), (gu_hbm, gu), (w_hbm, scr), (fwd_hbm, fwd_ref), (inv_hbm, inv_ref)]
         )
     ]
     loads[0].start()
@@ -112,8 +112,8 @@
         for j in range(local):
             shift(j).start()
 
-    loads[2].start()
-    loads[3].start()
+    for load in loads[2:]:
+        load.start()
     loads[0].wait()
     loads[1].wait()
 
@@ -125,8 +125,8 @@
         return carry
 
     lax.fori_loop(0, local, own_step, 0)
-    loads[2].wait()
-    loads[3].wait()
+    for load in loads[2:]:
+        load.wait()
 
     def take(j):
         pltpu.make_async_copy(
@@ -256,14 +256,15 @@
         forward, inverse = tables(groups, local)
         block = pltpu.VMEM(shape, BF16)
         dma = pltpu.SemaphoreType.DMA
-        anywhere = pl.BlockSpec(memory_space=pl.ANY)
-        vmem = pl.BlockSpec(memory_space=pltpu.VMEM)
+        anywhere = pl.BlockSpec(memory_space=pltpu.HBM)
         result = pl.pallas_call(
             functools.partial(kernel, groups, slices, halves),
             out_shape=jax.ShapeDtypeStruct(shape, BF16),
-            in_specs=[anywhere] * 4 + [vmem] * 2,
+            in_specs=[anywhere] * 6,
             out_specs=anywhere,
             scratch_shapes=[
+                pltpu.VMEM(forward.shape, BF16),
+                pltpu.VMEM(inverse.shape, BF16),
                 block, block, block, block, block,
                 pltpu.VMEM(shape, F32),
                 pltpu.VMEM((local, groups, 2, rows, size), BF16),
@@ -273,14 +274,14 @@
                 pltpu.VMEM((halves, local, groups, 2, part, size), BF16),
                 pltpu.VMEM((local, groups, halves, 2, part, size), BF16),
                 block,
-                dma((4,)),
+                dma((6,)),
                 dma((local,)), dma((local,)),
                 dma((local,)), dma((local,)),
                 dma((halves, local)), dma((halves, local)),
                 dma((local,)),
             ],
             compiler_params=pltpu.CompilerParams(
-                collective_id=0, has_side_effects=True, vmem_limit_bytes=48 * 1024 * 1024
+                collective_id=0, has_side_effects=True, vmem_limit_bytes=60 * 1024 * 1024
             ),
         )(
             green_diag[0], green_upper[0], sigma_lesser[0], screening[0],

time: 60.8 us -> 56.3 us (0.926)
  local copies, waits for them, and re-layouts: 7.38 us -> 2.26 us
  Pallas kernels: 53 us -> 53.9 us
    unnamed x13 -> x1, local copies, waits for them, and re-layouts: 7.38 us -> 2.26 us
    pallas_call x1, Pallas kernels: 53 us -> 53.9 us  [shards(): pl.pallas_call(functools.partial(kernel, groups, slices, halves), out_sha...]
where the time goes in v2:
time: 56.3 us; the launch traced here: 56.2 us
  Pallas kernels  53.9 us (96%)
  local copies, waits for them, and re-layouts  2.26 us (4%)
    pallas_call x1, Pallas kernels, shards(): pl.pallas_call(functools.partial(kernel, groups, slices, halves), out_sha...  53.9 us
    unnamed x1, local copies, waits for them, and re-layouts  2.26 us

profile of v2, /device:TPU:0, one launch (start us, length us, event | category | flops | bytes accessed | tf_op | source)
XLA Modules:
  0.0 56.2 jit_solution(7456433159490360850)
XLA Ops:
  0.0 53.9 %shard_map.64 = bf16[4,2,256,256]{3,2,1,0:T(8,128)(2,1)} custom-call(bf16[4,2,256,256]{3,2,1,0:T(8,128)(2,1)} %bitcast.6, bf16[4,2,256,256]{3,2,1,0:T(8,128)(2,1)} %bitcast.7, bf16[4,2,256,256]{3,2,1,0:T(8,128)(2,1)} %bitcast.8, bf16[4,2,256,256]{3,2,1,0:T(8,128)(2,1)} %bitcast.9, bf16[128,128]{1,0:T(8,128)(2,1)} %constant.4.clone.fwd_hbm, ...), custom_call_target="tpu_custom_call" | custom-call | tf_op jit(solution)/shard_map/pallas_call | solution.py:260
  53.9 2.3 %copy.8 = bf16[1,4,2,256,256]{4,3,2,1,0:T(8,128)(2,1)} copy(bf16[1,4,2,256,256]{4,3,2,1,0:T(8,128)(2,1)} %bitcast.5) | data formatting | bytes 2097152

commit v3 on v2

--- a/solution.py
+++ b/solution.py
@@ -57,7 +57,7 @@
 
 
 def kernel(
-    groups, slices, halves,
+    groups, slices, parts,
     gd_hbm, gu_hbm, s_hbm, w_hbm, fwd_hbm, inv_hbm, out_hbm,
     fwd_ref, inv_ref,    gd, gu, sig, scr, snext, own, lbuf, entries, xf, pf, pbuf, back, obuf,
     in_sem, z_send, z_recv, a_send, a_recv, b_send, b_recv, o_sem,
@@ -66,9 +66,8 @@
     cut = lax.axis_index("cuts")
     local, _, size, _ = gd.shape
     rows = size // groups
-    part = rows // halves
+    part = rows // parts
     count = 2 * groups * local
-    slab = 2 * groups * rows
 
     barrier = pltpu.get_barrier_semaphore()
 
@@ -128,13 +127,18 @@
     for load in loads[2:]:
         load.wait()
 
-    def take(j):
-        pltpu.make_async_copy(
-            entries.at[j, pl.ds(0, groups - 1)], entries.at[j, pl.ds(0, groups - 1)], a_recv.at[j]
-        ).wait()
-        wide = entries[j].astype(F32).reshape(slab, size)
+    stretch = 2 * groups * part
+
+    def take(j, h):
+        landed = entries.at[j, h, pl.ds(0, groups - 1)]
+        pltpu.make_async_copy(landed, landed, a_recv.at[j, h]).wait()
+        wide = entries[j, h].astype(F32).reshape(stretch, size)
         for q in range(size // LANES):
-            xf[pl.ds(q * count * rows + j * slab, slab), :] = wide[:, q * LANES : (q + 1) * LANES]
+            at = q * count * rows + h * count * part + j * stretch
+            xf[pl.ds(at, stretch), :] = wide[:, q * LANES : (q + 1) * LANES]
+
+    def each_part(body):
+        lax.fori_loop(0, parts, lambda h, carry: (body(h), carry)[1], 0)
 
     def lesser_step(j, carry):
         @pl.when(cut < slices - 1)
@@ -146,38 +150,42 @@
             own[j, 1] += li
 
         for c in range(2):
-            value = own[j, c].astype(BF16).reshape(groups, rows, size)
-            lbuf[j, :, c] = value
-        entries[j, me] = lbuf[j, me]
-
-        def send(k, inner):
-            to = lax.rem(me + k, groups)
-            pltpu.make_async_remote_copy(
-                src_ref=lbuf.at[j, to], dst_ref=entries.at[j, me],
-                send_sem=a_send.at[j], recv_sem=a_recv.at[j],
-                device_id={"energy": to}, device_id_type=MESH,
-            ).start()
-            return inner
-
-        lax.fori_loop(1, groups, send, 0)
+            value = own[j, c].astype(BF16).reshape(groups, parts, part, size)
+            for h in range(parts):
+                lbuf[j, h, :, c] = value[:, h]
+
+        def spread(h):
+            def send(k, inner):
+                to = lax.rem(me + k, groups)
+                pltpu.make_async_remote_copy(
+                    src_ref=lbuf.at[j, h, to], dst_ref=entries.at[j, h, me],
+                    send_sem=a_send.at[j, h], recv_sem=a_recv.at[j, h],
+                    device_id={"energy": to}, device_id_type=MESH,
+                ).start()
+                return inner
+
+            lax.fori_loop(1, groups, send, 0)
+            entries[j, h, me] = lbuf[j, h, me]
+
+        each_part(spread)
 
         @pl.when(j > 0)
         def _():
-            take(j - 1)
+            each_part(lambda h: take(j - 1, h))
 
         return carry
 
     lax.fori_loop(0, local, lesser_step, 0)
-    take(local - 1)
 
     period = count
 
-    for h in range(halves):
+    def part_step(h, outer):
+        take(local - 1, h)
 
         def correlate(i, carry):
-            r = h * part + i
+            at = h * count * part + i
             x = jnp.concatenate(
-                [xf[pl.ds(q * count * rows + r, count, stride=rows), :] for q in range(size // LANES)],
+                [xf[pl.ds(q * count * rows + at, count, stride=part), :] for q in range(size // LANES)],
                 axis=1,
             ).astype(BF16)
             spec = dot(fwd_ref[...], jnp.concatenate([x, x], axis=0))
@@ -187,39 +195,49 @@
             low = (power - high.astype(F32)).astype(BF16)
             lag = dot(inv_ref[...], jnp.concatenate([high, low, high], axis=0))
             for q in range(size // LANES):
-                pf[pl.ds(q * count * rows + r, count, stride=rows), :] = lag[:, q * LANES : (q + 1) * LANES]
+                pf[pl.ds(q * count * rows + at, count, stride=part), :] = (
+                    lag[:, q * LANES : (q + 1) * LANES]
+                )
             return carry
 
-        lax.fori_loop(0, part, correlate, 0, unroll=4)
+        lax.fori_loop(0, part, correlate, 0, unroll=min(part, 4))
 
         def ship(j, carry):
             lags = jnp.concatenate(
-                [pf[pl.ds(q * count * rows + j * slab, slab), :] for q in range(size // LANES)], axis=1
+                [
+                    pf[pl.ds(q * count * rows + h * count * part + j * stretch, stretch), :]
+                    for q in range(size // LANES)
+                ],
+                axis=1,
             )
-            lags = lags.reshape(groups, 2, rows, size)[:, :, h * part : (h + 1) * part]
-            pbuf[h, j] = lags.astype(BF16)
-            back[j, me, h] = pbuf[h, j, me]
+            pbuf[h, j] = lags.reshape(groups, 2, part, size).astype(BF16)
 
             def send(k, inner):
                 to = lax.rem(me + k, groups)
                 pltpu.make_async_remote_copy(
-                    src_ref=pbuf.at[h, j, to], dst_ref=back.at[j, me, h],
+                    src_ref=pbuf.at[h, j, to], dst_ref=back.at[j, h, me],
                     send_sem=b_send.at[h, j], recv_sem=b_recv.at[h, j],
                     device_id={"energy": to}, device_id_type=MESH,
                 ).start()
                 return inner
 
             lax.fori_loop(1, groups, send, 0)
+            back[j, h, me] = pbuf[h, j, me]
             return carry
 
         lax.fori_loop(0, local, ship, 0)
+        return outer
+
+    lax.fori_loop(0, parts, part_step, 0)
 
     def result_step(j, carry):
-        for h in range(halves):
-            landed = back.at[j, pl.ds(0, groups - 1), h]
+        for h in range(parts):
+            landed = back.at[j, h, pl.ds(0, groups - 1)]
             pltpu.make_async_copy(landed, landed, b_recv.at[h, j]).wait()
-        pr = back[j, :, :, 0].reshape(size, size)
-        pi = back[j, :, :, 1].reshape(size, size)
+        pr, pi = (
+            jnp.stack([back[j, h, :, c] for h in range(parts)], axis=1).reshape(size, size)
+            for c in range(2)
+        )
         tr, ti = times(scr[j, 0], scr[j, 1], pr, pi)
         lr, li = times_adjoint(tr.astype(BF16), ti.astype(BF16), scr[j, 0], scr[j, 1])
         obuf[j, 0] = lr.astype(BF16)
@@ -235,9 +253,9 @@
             shift(j).wait_send()
 
     for j in range(local):
-        sent = lbuf.at[j, pl.ds(0, groups - 1)]
-        pltpu.make_async_copy(sent, sent, a_send.at[j]).wait()
-        for h in range(halves):
+        for h in range(parts):
+            sent = lbuf.at[j, h, pl.ds(0, groups - 1)]
+            pltpu.make_async_copy(sent, sent, a_send.at[j, h]).wait()
             sent = pbuf.at[h, j, pl.ds(0, groups - 1)]
             pltpu.make_async_copy(sent, sent, b_send.at[h, j]).wait()
         pltpu.make_async_copy(obuf.at[j], out_hbm.at[j], o_sem.at[j]).wait()
@@ -250,15 +268,15 @@
         shape = green_diag.shape[1:]
         local, _, size, _ = shape
         rows = size // groups
-        halves = max(1, rows // 16)
-        part = rows // halves
+        parts = max(1, rows // 8)
+        part = rows // parts
         count = 2 * groups * local
         forward, inverse = tables(groups, local)
         block = pltpu.VMEM(shape, BF16)
         dma = pltpu.SemaphoreType.DMA
         anywhere = pl.BlockSpec(memory_space=pltpu.HBM)
         result = pl.pallas_call(
-            functools.partial(kernel, groups, slices, halves),
+            functools.partial(kernel, groups, slices, parts),
             out_shape=jax.ShapeDtypeStruct(shape, BF16),
             in_specs=[anywhere] * 6,
             out_specs=anywhere,
@@ -267,17 +285,17 @@
                 pltpu.VMEM(inverse.shape, BF16),
                 block, block, block, block, block,
                 pltpu.VMEM(shape, F32),
-                pltpu.VMEM((local, groups, 2, rows, size), BF16),
-                pltpu.VMEM((local, groups, 2, rows, size), BF16),
+                pltpu.VMEM((local, parts, groups, 2, part, size), BF16),
+                pltpu.VMEM((local, parts, groups, 2, part, size), BF16),
                 pltpu.VMEM((size // LANES * count * rows, LANES), F32),
                 pltpu.VMEM((size // LANES * count * rows, LANES), F32),
-                pltpu.VMEM((halves, local, groups, 2, part, size), BF16),
-                pltpu.VMEM((local, groups, halves, 2, part, size), BF16),
+                pltpu.VMEM((parts, local, groups, 2, part, size), BF16),
+                pltpu.VMEM((local, parts, groups, 2, part, size), BF16),
                 block,
                 dma((6,)),
                 dma((local,)), dma((local,)),
-                dma((local,)), dma((local,)),
-                dma((halves, local)), dma((halves, local)),
+                dma((local, parts)), dma((local, parts)),
+                dma((parts, local)), dma((parts, local)),
                 dma((local,)),
             ],
             compiler_params=pltpu.CompilerParams(

time: 56.3 us -> 53.2 us (0.945)
  Pallas kernels: 53.9 us -> 50.8 us
    pallas_call x1, Pallas kernels: 53.9 us -> 50.8 us  [shards(): pl.pallas_call(functools.partial(kernel, groups, slices, parts), out_shap...]
where the time goes in v3:
time: 53.2 us; the launch traced here: 53.1 us
  Pallas kernels  50.8 us (95%)
  local copies, waits for them, and re-layouts  2.26 us (4%)
    pallas_call x1, Pallas kernels, shards(): pl.pallas_call(functools.partial(kernel, groups, slices, parts), out_shap...  50.8 us
    unnamed x1, local copies, waits for them, and re-layouts  2.26 us

profile of v3, /device:TPU:0, one launch (start us, length us, event | category | flops | bytes accessed | tf_op | source)
XLA Modules:
  0.0 53.1 jit_solution(16658949284947713124)
XLA Ops:
  0.0 50.8 %shard_map.64 = bf16[4,2,256,256]{3,2,1,0:T(8,128)(2,1)} custom-call(bf16[4,2,256,256]{3,2,1,0:T(8,128)(2,1)} %bitcast.6, bf16[4,2,256,256]{3,2,1,0:T(8,128)(2,1)} %bitcast.7, bf16[4,2,256,256]{3,2,1,0:T(8,128)(2,1)} %bitcast.8, bf16[4,2,256,256]{3,2,1,0:T(8,128)(2,1)} %bitcast.9, bf16[128,128]{1,0:T(8,128)(2,1)} %constant.4.clone.fwd_hbm, ...), custom_call_target="tpu_custom_call" | custom-call | tf_op jit(solution)/shard_map/pallas_call | solution.py:278
  50.8 2.3 %copy.8 = bf16[1,4,2,256,256]{4,3,2,1,0:T(8,128)(2,1)} copy(bf16[1,4,2,256,256]{4,3,2,1,0:T(8,128)(2,1)} %bitcast.5) | data formatting | bytes 2097152

commit v4 on v3

--- a/solution.py
+++ b/solution.py
@@ -59,8 +59,8 @@
 def kernel(
     groups, slices, parts,
     gd_hbm, gu_hbm, s_hbm, w_hbm, fwd_hbm, inv_hbm, out_hbm,
-    fwd_ref, inv_ref,    gd, gu, sig, scr, snext, own, lbuf, entries, xf, pf, pbuf, back, obuf,
-    in_sem, z_send, z_recv, a_send, a_recv, b_send, b_recv, o_sem,
+    fwd_ref, inv_ref,    gd, gu, sig, scr, snext, loan, own, lbuf, entries, xf, pf, pbuf, back, obuf,
+    in_sem, z_send, z_recv, l_sem, a_send, a_recv, b_send, b_recv, o_sem,
 ):
     me = lax.axis_index("energy")
     cut = lax.axis_index("cuts")
@@ -71,6 +71,10 @@
 
     barrier = pltpu.get_barrier_semaphore()
 
+    first = lax.rem(me, 2)
+    partner = me + 1 - 2 * first
+    last = local - 1
+
     def greet(k, carry):
         pl.semaphore_signal(
             barrier, inc=1, device_id={"energy": lax.rem(me + k, groups)}, device_id_type=MESH
@@ -79,11 +83,17 @@
 
     @pl.when(cut > 0)
     def _():
-        pl.semaphore_signal(barrier, inc=1, device_id={"cuts": cut - 1}, device_id_type=MESH)
+        for who in (me, partner):
+            pl.semaphore_signal(
+                barrier, inc=1, device_id={"energy": who, "cuts": cut - 1}, device_id_type=MESH
+            )
 
     @pl.when(cut < slices - 1)
     def _():
-        pl.semaphore_signal(barrier, inc=1, device_id={"cuts": cut + 1}, device_id_type=MESH)
+        for who in (me, partner):
+            pl.semaphore_signal(
+                barrier, inc=1, device_id={"energy": who, "cuts": cut + 1}, device_id_type=MESH
+            )
 
     lax.fori_loop(1, groups, greet, 0)
 
@@ -97,19 +107,52 @@
     loads[1].start()
 
     edges = jnp.where(cut > 0, 1, 0) + jnp.where(cut < slices - 1, 1, 0)
-    pl.semaphore_wait(barrier, groups - 1 + edges)
+    pl.semaphore_wait(barrier, groups - 1 + 2 * edges)
 
     def shift(j):
         return pltpu.make_async_remote_copy(
             src_ref=s_hbm.at[j], dst_ref=snext.at[j],
             send_sem=z_send.at[j], recv_sem=z_recv.at[j],
-            device_id={"cuts": cut - 1}, device_id_type=MESH,
+            device_id={"energy": me, "cuts": cut - 1}, device_id_type=MESH,
+        )
+
+    def lend():
+        return pltpu.make_async_remote_copy(
+            src_ref=s_hbm.at[last, 1 - first], dst_ref=loan,
+            send_sem=l_sem.at[0], recv_sem=l_sem.at[1],
+            device_id={"energy": partner, "cuts": cut}, device_id_type=MESH,
+        )
+
+    def shift_mine():
+        return pltpu.make_async_remote_copy(
+            src_ref=s_hbm.at[last, first], dst_ref=snext.at[last, first],
+            send_sem=z_send.at[last], recv_sem=z_recv.at[last],
+            device_id={"energy": me, "cuts": cut - 1}, device_id_type=MESH,
+        )
+
+    def shift_loan():
+        return pltpu.make_async_remote_copy(
+            src_ref=loan, dst_ref=snext.at[last, first],
+            send_sem=z_send.at[local], recv_sem=z_recv.at[local],
+            device_id={"energy": partner, "cuts": cut - 1}, device_id_type=MESH,
         )
 
     @pl.when(cut > 0)
     def _():
-        for j in range(local):
+        lend().start()
+        for j in range(last):
             shift(j).start()
+        lend().wait_recv()
+
+        @pl.when(first == 0)
+        def _():
+            shift_mine().start()
+            shift_loan().start()
+
+        @pl.when(first == 1)
+        def _():
+            shift_loan().start()
+            shift_mine().start()
 
     for load in loads[2:]:
         load.start()
@@ -143,7 +186,15 @@
     def lesser_step(j, carry):
         @pl.when(cut < slices - 1)
         def _():
-            shift(j).wait_recv()
+            @pl.when(j < last)
+            def _():
+                shift(j).wait_recv()
+
+            @pl.when(j == last)
+            def _():
+                shift_mine().wait_recv()
+                shift_loan().wait_recv()
+
             tr, ti = times(gu[j, 0], gu[j, 1], snext[j, 0], snext[j, 1])
             lr, li = times_adjoint(tr.astype(BF16), ti.astype(BF16), gu[j, 0], gu[j, 1])
             own[j, 0] += lr
@@ -249,8 +300,11 @@
 
     @pl.when(cut > 0)
     def _():
-        for j in range(local):
+        for j in range(last):
             shift(j).wait_send()
+        shift_mine().wait_send()
+        shift_loan().wait_send()
+        lend().wait_send()
 
     for j in range(local):
         for h in range(parts):
@@ -284,6 +338,7 @@
                 pltpu.VMEM(forward.shape, BF16),
                 pltpu.VMEM(inverse.shape, BF16),
                 block, block, block, block, block,
+                pltpu.VMEM(shape[2:], BF16),
                 pltpu.VMEM(shape, F32),
                 pltpu.VMEM((local, parts, groups, 2, part, size), BF16),
                 pltpu.VMEM((local, parts, groups, 2, part, size), BF16),
@@ -293,7 +348,7 @@
                 pltpu.VMEM((local, parts, groups, 2, part, size), BF16),
                 block,
                 dma((6,)),
-                dma((local,)), dma((local,)),
+                dma((local + 1,)), dma((local + 1,)), dma((2,)),
                 dma((local, parts)), dma((local, parts)),
                 dma((parts, local)), dma((parts, local)),
                 dma((local,)),

time: 53.2 us -> 52.4 us (0.985)
  Pallas kernels: 50.8 us -> 50 us
    pallas_call x1, Pallas kernels: 50.8 us -> 50 us  [shards(): pl.pallas_call(functools.partial(kernel, groups, slices, parts), out_shap...]
where the time goes in v4:
time: 52.4 us; the launch traced here: 52.2 us
  Pallas kernels  50 us (95%)
  local copies, waits for them, and re-layouts  2.26 us (4%)
    pallas_call x1, Pallas kernels, shards(): pl.pallas_call(functools.partial(kernel, groups, slices, parts), out_shap...  50 us
    unnamed x1, local copies, waits for them, and re-layouts  2.26 us

profile of v4, /device:TPU:0, one launch (start us, length us, event | category | flops | bytes accessed | tf_op | source)
XLA Modules:
  0.0 52.2 jit_solution(9818289853241261410)
XLA Ops:
  0.0 50.0 %shard_map.64 = bf16[4,2,256,256]{3,2,1,0:T(8,128)(2,1)} custom-call(bf16[4,2,256,256]{3,2,1,0:T(8,128)(2,1)} %bitcast.6, bf16[4,2,256,256]{3,2,1,0:T(8,128)(2,1)} %bitcast.7, bf16[4,2,256,256]{3,2,1,0:T(8,128)(2,1)} %bitcast.8, bf16[4,2,256,256]{3,2,1,0:T(8,128)(2,1)} %bitcast.9, bf16[128,128]{1,0:T(8,128)(2,1)} %constant.4.clone.fwd_hbm, ...), custom_call_target="tpu_custom_call" | custom-call | tf_op jit(solution)/shard_map/pallas_call | solution.py:332
  50.0 2.3 %copy.8 = bf16[1,4,2,256,256]{4,3,2,1,0:T(8,128)(2,1)} copy(bf16[1,4,2,256,256]{4,3,2,1,0:T(8,128)(2,1)} %bitcast.5) | data formatting | bytes 2097152

commit v5 on v4

--- a/solution.py
+++ b/solution.py
@@ -1,8 +1,8 @@
 import functools
+import math
 
 import jax
 import jax.numpy as jnp
-import numpy as np
 from jax import lax
 from jax.experimental import pallas as pl
 from jax.experimental.pallas import tpu as pltpu
@@ -14,30 +14,38 @@
 BF16 = jnp.bfloat16
 
 
-def tables(groups, local):
+def fill_tables(fwd_ref, inv_ref, groups, local):
     energies = groups * local
     period = 2 * energies
-    order = np.array([s * local + j for j in range(local) for s in range(groups)])
-    freq = np.arange(period)
-    angle = 2.0 * np.pi * ((freq[:, None] * order[None, :]) % period) / period
-    cos, sin = np.cos(angle), np.sin(angle)
-    forward = np.zeros((2 * period, energies, 2))
-    forward[:period, :, 0], forward[:period, :, 1] = cos, sin
-    forward[period:, :, 0], forward[period:, :, 1] = -sin, cos
-    forward = forward.reshape(2 * period, 2 * energies).astype(np.float32)
-    inverse = np.stack([cos.T, sin.T], axis=1).reshape(2 * energies, period)
-    inverse = (inverse / (period * energies)).astype(np.float32)
+    rest = 2 * groups
+
+    def index(shape, axis):
+        return lax.broadcasted_iota(jnp.int32, shape, axis)
+
+    def point(position):
+        device = lax.div(lax.rem(position, rest), 2)
+        return device * local + lax.div(position, rest), lax.rem(position, 2)
+
+    def cosine(phase, quarters):
+        phase = lax.rem(phase + quarters * (period // 4), period)
+        return jnp.cos(phase.astype(F32) * (2.0 * math.pi / period))
 
     def split(table):
         high = table.astype(BF16)
-        return high, (table - high.astype(np.float32)).astype(BF16)
-
-    f_high, f_low = split(forward)
-    i_high, i_low = split(inverse)
-    return (
-        np.concatenate([f_high, f_low], axis=1),
-        np.concatenate([i_high, i_high, i_low], axis=1),
-    )
+        return high, (table - high.astype(F32)).astype(BF16)
+
+    shape = (2 * period, period)
+    energy, component = point(index(shape, 1))
+    row = index(shape, 0)
+    table = cosine(lax.rem(row, period) * energy, lax.div(row, period) + 4 - component)
+    high, low = split(table)
+    fwd_ref[...] = jnp.concatenate([high, low], axis=1)
+
+    shape = (period, period)
+    lag, component = point(index(shape, 0))
+    table = cosine(lag * index(shape, 1), 4 - component) * (1.0 / (period * energies))
+    high, low = split(table)
+    inv_ref[...] = jnp.concatenate([high, high, low], axis=1)
 
 
 def dot(left, right):
@@ -58,7 +66,7 @@
 
 def kernel(
     groups, slices, parts,
-    gd_hbm, gu_hbm, s_hbm, w_hbm, fwd_hbm, inv_hbm, out_hbm,
+    gd_hbm, gu_hbm, s_hbm, w_hbm, out_hbm,
     fwd_ref, inv_ref,    gd, gu, sig, scr, snext, loan, own, lbuf, entries, xf, pf, pbuf, back, obuf,
     in_sem, z_send, z_recv, l_sem, a_send, a_recv, b_send, b_recv, o_sem,
 ):
@@ -100,7 +108,7 @@
     loads = [
         pltpu.make_async_copy(source, target, in_sem.at[i])
         for i, (source, target) in enumerate(
-            [(gd_hbm, gd), (s_hbm, sig), (gu_hbm, gu), (w_hbm, scr), (fwd_hbm, fwd_ref), (inv_hbm, inv_ref)]
+            [(gd_hbm, gd), (s_hbm, sig), (gu_hbm, gu), (w_hbm, scr)]
         )
     ]
     loads[0].start()
@@ -156,6 +164,7 @@
 
     for load in loads[2:]:
         load.start()
+    fill_tables(fwd_ref, inv_ref, groups, local)
     loads[0].wait()
     loads[1].wait()
 
@@ -325,18 +334,17 @@
         parts = max(1, rows // 8)
         part = rows // parts
         count = 2 * groups * local
-        forward, inverse = tables(groups, local)
         block = pltpu.VMEM(shape, BF16)
         dma = pltpu.SemaphoreType.DMA
         anywhere = pl.BlockSpec(memory_space=pltpu.HBM)
         result = pl.pallas_call(
             functools.partial(kernel, groups, slices, parts),
             out_shape=jax.ShapeDtypeStruct(shape, BF16),
-            in_specs=[anywhere] * 6,
-            out_specs=anywhere,
+            in_specs=[anywhere] * 4,
+            out_specs=pl.BlockSpec(memory_space=pl.ANY),
             scratch_shapes=[
-                pltpu.VMEM(forward.shape, BF16),
-                pltpu.VMEM(inverse.shape, BF16),
+                pltpu.VMEM((2 * count, 2 * count), BF16),
+                pltpu.VMEM((count, 3 * count), BF16),
                 block, block, block, block, block,
                 pltpu.VMEM(shape[2:], BF16),
                 pltpu.VMEM(shape, F32),
@@ -347,18 +355,17 @@
                 pltpu.VMEM((parts, local, groups, 2, part, size), BF16),
                 pltpu.VMEM((local, parts, groups, 2, part, size), BF16),
                 block,
-                dma((6,)),
+                dma((4,)),
                 dma((local + 1,)), dma((local + 1,)), dma((2,)),
                 dma((local, parts)), dma((local, parts)),
                 dma((parts, local)), dma((parts, local)),
                 dma((local,)),
             ],
             compiler_params=pltpu.CompilerParams(
-                collective_id=0, has_side_effects=True, vmem_limit_bytes=60 * 1024 * 1024
+                collective_id=0, has_side_effects=True, vmem_limit_bytes=54525952
             ),
         )(
-            green_diag[0], green_upper[0], sigma_lesser[0], screening[0],
-            jnp.asarray(forward), jnp.asarray(inverse),
+            green_diag[0], green_upper[0], sigma_lesser[0], screening[0]
         )
         return result[None]
 

time: 52.4 us -> 50.5 us (0.964)
  local copies, waits for them, and re-layouts: 2.26 us -> 0.97 us
  Pallas kernels: 50 us -> 49.4 us
    unnamed x1, local copies, waits for them, and re-layouts: 2.26 us -> 0.97 us
    pallas_call x1, Pallas kernels: 50 us -> 49.4 us  [shards(): pl.pallas_call(functools.partial(kernel, groups, slices, parts), out_shap...]
where the time goes in v5:
time: 50.5 us; the launch traced here: 50.3 us
  Pallas kernels  49.4 us (98%)
  local copies, waits for them, and re-layouts  0.97 us (2%)
    pallas_call x1, Pallas kernels, shards(): pl.pallas_call(functools.partial(kernel, groups, slices, parts), out_shap...  49.4 us

profile of v5, /device:TPU:0, one launch (start us, length us, event | category | flops | bytes accessed | tf_op | source)
XLA Modules:
  0.0 50.3 jit_solution(6192780817947149768)
XLA Ops:
  0.0 49.4 %shard_map.46 = bf16[4,2,256,256]{3,2,1,0:T(8,128)(2,1)S(1)} custom-call(bf16[4,2,256,256]{3,2,1,0:T(8,128)(2,1)} %bitcast.6, bf16[4,2,256,256]{3,2,1,0:T(8,128)(2,1)} %bitcast.7, bf16[4,2,256,256]{3,2,1,0:T(8,128)(2,1)} %bitcast.8, bf16[4,2,256,256]{3,2,1,0:T(8,128)(2,1)} %bitcast.9), custom_call_target="tpu_custom_call" | custom-call | tf_op jit(solution)/shard_map/pallas_call | solution.py:340
  49.4 1.0 %copy.6 = bf16[1,4,2,256,256]{4,3,2,1,0:T(8,128)(2,1)} copy(bf16[1,4,2,256,256]{4,3,2,1,0:T(8,128)(2,1)S(1)} %bitcast.5) | data formatting | bytes 2097152
